TPU v7x, 32 devices: a whole 2x2x4 slice. The times are simulated.
32 devices in a mesh: dp: 8 (over y, x, core), shard: 4 (over z).
Axes of the slice: x: 2, y: 2, z: 4, core: 2. Of those that a mesh axis runs over, the one named last changes fastest.
Arguments:
- activations: bfloat16 [4096, 4096], P('dp', 'shard'), may hold values from -6 to 6
- out_grads: bfloat16 [4096, 14336], P('dp', 'shard'), may hold values from -6 to 6
- sign_bits: int32 [14336], P('shard'), may hold values from 0 to 1
- block_ids: int32 [4, 8], replicated, may hold values from 0 to 111, as said below
Outputs:
- gram: float32 [4096, 1024], P('shard')
Inputs may be any that keep to these rules, and one draw needn't show every extreme that they name: `block_ids`: row o holds 4 runs of 2 entries; the entries of a run are distinct blocks of one shard s (ids s * 28 + 0 to s * 28 + 27), and the runs of a row come from distinct shards.
All inputs are finite; a program needn't handle non-finite values.
Results may differ from a plain program's by a relative error of at most 0.006.
Values may be sent and summed in bfloat16 or wider, within the bound.
A program may use at most 64 MiB of HBM per device.

v0:
```python
import math
import jax
import jax.numpy as jnp
from jax import lax
from jax.sharding import PartitionSpec as P

BLK = 128
CAP = 2


def partner_2(x, axis, distance):
    return lax.ppermute(x, axis, [(i, i ^ 1 << distance) for i in range(lax.axis_size(axis))])


def parity_table(count):
    index = jnp.arange(count, dtype=jnp.int32)
    total = jnp.zeros((count, count), jnp.int32)
    for level in range(count.bit_length() - 1):
        total = total + (
            jnp.right_shift(index[:, None], level) & jnp.right_shift(index[None, :], level) & 1
        )
    return (1 - 2 * (total % 2)).astype(jnp.float32)


def route_sampled(mixed, block_ids, me_index, shards, blocks_per, tokens, width):
    groups = block_ids.shape[1] // CAP
    sources = block_ids[:, ::CAP] // blocks_per
    local_ids = (block_ids % blocks_per).reshape(shards, groups, CAP)
    matched = sources == me_index
    chosen = jnp.sum(jnp.where(matched[:, :, None], local_ids, 0), axis=1)
    live_rows = jnp.any(matched, axis=1).astype(jnp.bfloat16)
    outgoing = jnp.take(mixed, chosen.reshape(-1), axis=0).reshape(shards, CAP, tokens, width)
    return (outgoing * live_rows[:, None, None, None], jnp.take(sources, me_index, axis=0))


def body(activations, out_grads, sign_bits, block_ids):
    shards = lax.axis_size("shard")
    me_index = lax.axis_index("shard")
    tokens = out_grads.shape[0]
    width = BLK
    own_blocks = block_ids.shape[1]
    blocks_per = out_grads.shape[1] // width
    model_width = activations.shape[1] * shards
    inv_block = 1.0 / math.sqrt(width)
    inv_shard = 1.0 / math.sqrt(shards)
    partial_gram = jnp.dot(activations, activations.T, preferred_element_type=jnp.float32)
    token_gram = lax.psum(partial_gram, "shard").astype(jnp.bfloat16)
    sign_values = (1 - 2 * sign_bits).astype(jnp.bfloat16)
    flipped = (out_grads * sign_values[None, :]).reshape(tokens, blocks_per, width)
    block_table = parity_table(width).astype(jnp.bfloat16)
    local_mix = jnp.einsum("tbj,jk->btk", flipped, block_table, preferred_element_type=jnp.float32)
    local_mix = (local_mix * inv_block).astype(jnp.bfloat16)
    running = local_mix.astype(jnp.float32)
    for level in range(shards.bit_length() - 1):
        partner = partner_2(running, "shard", level)
        upper = jnp.right_shift(me_index, level) & 1 == 1
        running = jnp.where(upper, partner - running, running + partner)
    mixed = (running * inv_shard).astype(jnp.bfloat16)
    outgoing, own_sources = route_sampled(
        mixed, block_ids, me_index, shards, blocks_per, tokens, width
    )
    incoming = lax.all_to_all(outgoing, "shard", split_axis=0, concat_axis=0, tiled=True)
    sketched = jnp.take(incoming, own_sources, axis=0).reshape(own_blocks, tokens, width)
    weighted = jnp.einsum(
        "tu,jub->jtb", token_gram, sketched, preferred_element_type=jnp.float32
    ).astype(jnp.bfloat16)
    block_gram = jnp.einsum("jtb,ktc->jbkc", sketched, weighted, preferred_element_type=jnp.float32)
    own_cols = own_blocks * width
    block_gram = block_gram.reshape(own_cols, own_cols)
    summed = lax.psum(block_gram, "dp")
    return summed / (lax.axis_size("dp") * tokens * model_width)


def solution(mesh):
    in_specs = (P("dp", "shard"), P("dp", "shard"), P("shard"), P())
    out_specs = P("shard", None)
    return jax.shard_map(body, mesh=mesh, in_specs=in_specs, out_specs=out_specs, check_vma=False)
```

profile of v0, /device:TPU:0, one launch (start us, length us, event | category | flops | bytes accessed | tf_op | source)
XLA Modules:
  0.0 690.9 jit_solution(8151458818415333310)
XLA Ops:
  6.6 6.0 copy.15
  12.6 0.0 copy-done.1
  12.6 3.3 broadcast_multiply_fusion.1
  15.9 4.3 convert_bitcast_fusion
  20.2 3.1 collective-permute-start
  23.3 158.3 %collective-permute-done = f32[28,512,128]{1,2,0:T(8,128)} collective-permute-done((f32[28,512,128]{1,2,0:T(8,128)}, f32[28,512,128]{1,2,0:T(8,128)}, u32[]{:S(2)}, u32[]{:S(2)}) %collective-permute-start) | collective-permute-done | bytes 7340064 | tf_op jit(solution)/shard_map/ppermute | solution.py:12
  181.6 10.6 %add_select_fusion = f32[28,512,128]{1,2,0:T(8,128)} fusion(f32[28,512,128]{1,2,0:T(8,128)} %convert_bitcast_fusion, f32[28,512,128]{1,2,0:T(8,128)} %collective-permute-done, pred[]{:T(512)S(6)} %eq.19), kind=kLoop, calls=%fused_computation.4 | loop fusion | flops 5505024 | bytes 22020096 | tf_op jit(solution)/shard_map/jit(_where)/select_n | solution.py:57
  192.1 2.8 collective-permute-start.1
  194.9 0.1 slice.3
  195.0 0.1 copy.13
  195.1 0.1 fusion.32
  195.2 0.1 copy.12
  195.3 0.1 copy.17
  195.4 0.1 reshape.154
  195.5 0.1 copy.14
  195.7 0.1 broadcast_in_dim.63
  195.7 0.1 broadcast_in_dim.64
  195.8 314.0 %collective-permute-done.1 = f32[28,512,128]{1,2,0:T(8,128)} collective-permute-done((f32[28,512,128]{1,2,0:T(8,128)}, f32[28,512,128]{1,2,0:T(8,128)}, u32[]{:S(2)}, u32[]{:S(2)}) %collective-permute-start.1) | collective-permute-done | bytes 7340064 | tf_op jit(solution)/shard_map/ppermute | solution.py:12
  509.8 9.1 %multiply_convert_fusion = bf16[28,512,128]{1,2,0:T(8,128)(2,1)} fusion(f32[28,512,128]{1,2,0:T(8,128)} %add_select_fusion, f32[28,512,128]{1,2,0:T(8,128)} %collective-permute-done.1, pred[]{:T(512)S(6)} %eq.18), kind=kLoop, calls=%fused_computation.3 | loop fusion | flops 9175040 | bytes 18350080 | tf_op jit(solution)/shard_map/convert_element_type | solution.py:58
  518.9 2.6 gather_fusion
  521.5 1.1 select_multiply_fusion
  522.7 4.6 all-to-all-start
  527.3 0.7 fusion.33
  528.1 63.9 %all-reduce.4 = bf16[512,512]{1,0:T(8,128)(2,1)} all-reduce(f32[512,512]{1,0:T(8,128)S(1)} %fusion.33), channel_id=1, replica_groups=mesh['dp'=8,'shard'=4] {'shard'}, use_global_device_ids=true, to_apply=%region_2.3 | all-reduce | flops 262144 | bytes 1572864 | tf_op jit(solution)/shard_map/psum | solution.py:47
  591.9 0.0 all-to-all-done
  591.9 0.6 gather_fusion.1
  592.6 0.2 bitcast_select_fusion
  592.7 1.8 convolution_convert_fusion
  594.5 3.3 fusion.34
  597.8 0.0 all-reduce.3.cloned.1.call-update
  597.8 81.2 %all-reduce.3.cloned.1.call-done = f32[1024,1024]{1,0:T(8,128)} async-done(((f32[1024,1024]{1,0:T(8,128)}), f32[1024,1024]{1,0:T(8,128)}) %all-reduce.3.cloned.1.call-update) | async-done | bytes 4194320 | tf_op jit(solution)/shard_map/psum | solution.py:70
  679.0 5.0 broadcast_multiply_fusion
  (20 shorter events, 0.1 us)
Async XLA Ops:
  6.5 520.8 %copy-start = (bf16[512,1024]{1,0:T(8,128)(2,1)S(1)}, bf16[512,1024]{1,0:T(8,128)(2,1)}, u32[]{:S(2)}) copy-start(bf16[512,1024]{1,0:T(8,128)(2,1)} %param.4) | copy-start | bytes 3145732
  6.5 6.0 copy-start.1
  20.2 161.4 %collective-permute-start = (f32[28,512,128]{1,2,0:T(8,128)}, f32[28,512,128]{1,2,0:T(8,128)}, u32[]{:S(2)}, u32[]{:S(2)}) collective-permute-start(f32[28,512,128]{1,2,0:T(8,128)} %convert_bitcast_fusion), channel_id=1, source_target_pairs={{0,1},{1,0},{2,3},{3,2},{4,5},{5,4},{6,7},{7,6},{8,9},{9,8},{10,11... | collective-permute-start | bytes 22020104 | tf_op jit(solution)/shard_map/ppermute | solution.py:12
  23.3 171.6 %copy-start.2 = (s32[4,8]{1,0:T(4,128)S(1)}, s32[4,8]{1,0:T(4,128)}, u32[]{:S(2)}) copy-start(s32[4,8]{1,0:T(4,128)} %param.7) | copy-start | bytes 388
  192.1 317.7 %collective-permute-start.1 = (f32[28,512,128]{1,2,0:T(8,128)}, f32[28,512,128]{1,2,0:T(8,128)}, u32[]{:S(2)}, u32[]{:S(2)}) collective-permute-start(f32[28,512,128]{1,2,0:T(8,128)} %add_select_fusion), channel_id=1, source_target_pairs={{0,2},{1,3},{2,0},{3,1},{4,6},{5,7},{6,4},{7,5},{8,10},{9,11},{10,... | collective-permute-start | bytes 22020104 | tf_op jit(solution)/shard_map/ppermute | solution.py:12
  522.7 69.3 %all-to-all-start = ((bf16[4,2,512,128]{2,3,1,0:T(8,128)(2,1)}), bf16[4,2,512,128]{2,3,1,0:T(8,128)(2,1)S(1)}, u32[]{:S(2)}, u32[]{:S(2)}) async-start(bf16[4,2,512,128]{2,3,1,0:T(8,128)(2,1)} %select_multiply_fusion), calls=%async_computation | async-start | bytes 2097152 | tf_op jit(solution)/shard_map/all_to_all | solution.py:62
  527.3 151.7 %all-reduce.3.cloned.1.call-start = ((), (), s32[]{:S(2)}) async-start(), calls=%async_computation.1 | async-start | bytes 8388608 | tf_op jit(solution)/shard_map/psum | solution.py:70
Sparse Core Ops, SparseCore 0:
  598.0 80.9 all-reduce.2
where the time goes:
time: 691 us
  waiting for transfers between devices  553 us (80%)
  blocking collectives  63.9 us (9%)
  other arithmetic  29.5 us (4%)
  between operations  13.5 us (2%)
  starting transfers between devices  10.5 us (2%)
  matrix products  10.1 us (1%)
  local copies, waits for them, and re-layouts  10 us (1%)
    ppermute x2, waiting for transfers between devices, partner_2(): lax.ppermute(x, axis, [(i, i ^ 1 << distance) for i in range(lax.axis_siz...  472 us
    psum x1, waiting for transfers between devices, body(): summed = lax.psum(block_gram, 'dp')  81.2 us
    psum x1, blocking collectives, body(): token_gram = lax.psum(partial_gram, 'shard').astype(jnp.bfloat16)  63.9 us
  transfers between devices with their start and end apart: 4, of which 3 were waited for; matrix products, arithmetic and copies ran while one was open for 0% of the time, Pallas kernels for 0%

commit v1 on v0

--- a/solution.py
+++ b/solution.py
@@ -67,7 +67,7 @@
     block_gram = jnp.einsum("jtb,ktc->jbkc", sketched, weighted, preferred_element_type=jnp.float32)
     own_cols = own_blocks * width
     block_gram = block_gram.reshape(own_cols, own_cols)
-    summed = lax.psum(block_gram, "dp")
+    summed = jnp.sum(lax.all_gather(block_gram, "dp"), axis=0)
     return summed / (lax.axis_size("dp") * tokens * model_width)
 
 

time: 691 us -> 786 us (1.14)
  waiting for transfers between devices: 553 us -> 633 us
  other arithmetic: 29.5 us -> 45 us
    all_gather x0 -> x1, waiting for transfers between devices: none -> 161 us  [body(): summed = jnp.sum(lax.all_gather(block_gram, 'dp'), axis=0)]
    psum x1 -> x0, waiting for transfers between devices: 81.2 us -> none  [body(): summed = lax.psum(block_gram, 'dp')]
    reduce_sum x0 -> x1, other arithmetic: none -> 14.7 us  [body(): summed = jnp.sum(lax.all_gather(block_gram, 'dp'), axis=0)]
where the time goes in v1:
time: 786 us; the launch traced here: 785 us
  waiting for transfers between devices  633 us (81%)
  blocking collectives  63.8 us (8%)
  other arithmetic  45 us (6%)
  between operations  13.5 us (2%)
  starting transfers between devices  10.5 us (1%)
  local copies, waits for them, and re-layouts  10.2 us (1%)
  matrix products  9.05 us (1%)
    ppermute x2, waiting for transfers between devices, partner_2(): lax.ppermute(x, axis, [(i, i ^ 1 << distance) for i in range(lax.axis_siz...  472 us
    all_gather x1, waiting for transfers between devices, body(): summed = jnp.sum(lax.all_gather(block_gram, 'dp'), axis=0)  161 us
    psum x1, blocking collectives, body(): token_gram = lax.psum(partial_gram, 'shard').astype(jnp.bfloat16)  63.8 us
  transfers between devices with their start and end apart: 4, of which 3 were waited for; matrix products, arithmetic and copies ran while one was open for 0% of the time, Pallas kernels for 0%

profile of v1, /device:TPU:0, one launch (start us, length us, event | category | flops | bytes accessed | tf_op | source)
XLA Modules:
  0.0 785.3 jit_solution(7929377771402737445)
XLA Ops:
  6.6 0.8 subtract_convert_fusion
  7.4 5.9 copy.15
  13.3 3.3 broadcast_multiply_fusion.1
  16.6 4.3 convert_bitcast_fusion
  20.9 3.1 collective-permute-start
  23.9 158.3 %collective-permute-done = f32[28,512,128]{1,2,0:T(8,128)} collective-permute-done((f32[28,512,128]{1,2,0:T(8,128)}, f32[28,512,128]{1,2,0:T(8,128)}, u32[]{:S(2)}, u32[]{:S(2)}) %collective-permute-start) | collective-permute-done | bytes 7340064 | tf_op jit(solution)/shard_map/ppermute | solution.py:12
  182.2 10.6 %add_select_fusion = f32[28,512,128]{1,2,0:T(8,128)} fusion(f32[28,512,128]{1,2,0:T(8,128)} %convert_bitcast_fusion, f32[28,512,128]{1,2,0:T(8,128)} %collective-permute-done, pred[]{:T(512)S(6)} %eq.19), kind=kLoop, calls=%fused_computation.4 | loop fusion | flops 5505024 | bytes 22020096 | tf_op jit(solution)/shard_map/jit(_where)/select_n | solution.py:57
  192.8 2.8 collective-permute-start.1
  195.5 0.1 slice.3
  195.6 0.1 copy.13
  195.7 0.1 fusion.32
  195.9 0.1 copy.12
  196.0 0.1 broadcast_in_dim.63
  196.1 0.1 broadcast_in_dim.64
  196.2 0.1 copy.17
  196.3 0.1 copy.14
  196.4 0.1 reshape.158
  196.5 313.9 %collective-permute-done.1 = f32[28,512,128]{1,2,0:T(8,128)} collective-permute-done((f32[28,512,128]{1,2,0:T(8,128)}, f32[28,512,128]{1,2,0:T(8,128)}, u32[]{:S(2)}, u32[]{:S(2)}) %collective-permute-start.1) | collective-permute-done | bytes 7340064 | tf_op jit(solution)/shard_map/ppermute | solution.py:12
  510.4 9.1 %multiply_convert_fusion = bf16[28,512,128]{1,2,0:T(8,128)(2,1)} fusion(f32[28,512,128]{1,2,0:T(8,128)} %add_select_fusion, f32[28,512,128]{1,2,0:T(8,128)} %collective-permute-done.1, pred[]{:T(512)S(6)} %eq.18), kind=kLoop, calls=%fused_computation.3 | loop fusion | flops 9175040 | bytes 18350080 | tf_op jit(solution)/shard_map/convert_element_type | solution.py:58
  519.5 2.6 gather_fusion
  522.1 1.1 select_multiply_fusion
  523.3 4.6 all-to-all-start
  527.9 0.7 fusion.33
  528.7 63.8 %all-reduce.1 = bf16[512,512]{1,0:T(8,128)(2,1)} all-reduce(f32[512,512]{1,0:T(8,128)S(1)} %fusion.33), channel_id=1, replica_groups=mesh['dp'=8,'shard'=4] {'shard'}, use_global_device_ids=true, to_apply=%region_2.3 | all-reduce | flops 262144 | bytes 1572864 | tf_op jit(solution)/shard_map/psum | solution.py:47
  592.6 0.6 gather_fusion.1
  593.2 0.2 bitcast_select_fusion
  593.4 0.2 copy-done.2
  593.6 0.7 convolution_convert_fusion
  594.3 3.3 fusion.34
  597.7 161.0 %all-gather.3.cloned.1.call-done = f32[8192,1024]{1,0:T(8,128)} async-done(((f32[1024,1024]{1,0:T(8,128)}), f32[8192,1024]{1,0:T(8,128)}) %all-gather.3.cloned.1.call-update) | async-done | bytes 33554448 | tf_op jit(solution)/shard_map/all_gather | solution.py:70
  758.7 14.7 %reduce_sum.19 = f32[1024,1024]{1,0:T(8,128)} reduce(f32[8,1024,1024]{2,1,0:T(8,128)} %bitcast.32, f32[]{:T(128)} %constant.111.clone.1), dimensions={0}, to_apply=%region_3.4 | reduce | flops 7340032 | bytes 37748740 | tf_op jit(solution)/shard_map/reduce_sum | solution.py:70
  773.4 5.0 broadcast_multiply_fusion
  (23 shorter events, 0.1 us)
Async XLA Ops:
  6.5 521.4 %copy-start = (bf16[512,1024]{1,0:T(8,128)(2,1)S(1)}, bf16[512,1024]{1,0:T(8,128)(2,1)}, u32[]{:S(2)}) copy-start(bf16[512,1024]{1,0:T(8,128)(2,1)} %param.4) | copy-start | bytes 3145732
  20.9 161.3 %collective-permute-start = (f32[28,512,128]{1,2,0:T(8,128)}, f32[28,512,128]{1,2,0:T(8,128)}, u32[]{:S(2)}, u32[]{:S(2)}) collective-permute-start(f32[28,512,128]{1,2,0:T(8,128)} %convert_bitcast_fusion), channel_id=1, source_target_pairs={{0,1},{1,0},{2,3},{3,2},{4,5},{5,4},{6,7},{7,6},{8,9},{9,8},{10,11... | collective-permute-start | bytes 22020104 | tf_op jit(solution)/shard_map/ppermute | solution.py:12
  23.9 171.6 %copy-start.3 = (s32[4,8]{1,0:T(4,128)S(1)}, s32[4,8]{1,0:T(4,128)}, u32[]{:S(2)}) copy-start(s32[4,8]{1,0:T(4,128)} %param.7) | copy-start | bytes 388
  192.8 317.7 %collective-permute-start.1 = (f32[28,512,128]{1,2,0:T(8,128)}, f32[28,512,128]{1,2,0:T(8,128)}, u32[]{:S(2)}, u32[]{:S(2)}) collective-permute-start(f32[28,512,128]{1,2,0:T(8,128)} %add_select_fusion), channel_id=1, source_target_pairs={{0,2},{1,3},{2,0},{3,1},{4,6},{5,7},{6,4},{7,5},{8,10},{9,11},{10,... | collective-permute-start | bytes 22020104 | tf_op jit(solution)/shard_map/ppermute | solution.py:12
  523.3 69.3 %all-to-all-start = ((bf16[4,2,512,128]{2,3,1,0:T(8,128)(2,1)}), bf16[4,2,512,128]{2,3,1,0:T(8,128)(2,1)S(1)}, u32[]{:S(2)}, u32[]{:S(2)}) async-start(bf16[4,2,512,128]{2,3,1,0:T(8,128)(2,1)} %select_multiply_fusion), calls=%async_computation | async-start | bytes 2097152 | tf_op jit(solution)/shard_map/all_to_all | solution.py:62
  527.9 230.8 %all-gather.3.cloned.1.call-start = ((), (), s32[]{:S(2)}) async-start(), calls=%async_computation.1 | async-start | bytes 37748736 | tf_op jit(solution)/shard_map/all_gather | solution.py:70
  592.6 1.0 copy-start.2
  758.7 19.8 %copy-start.1 = (bf16[512,1024]{1,0:T(8,128)(2,1)S(1)}, bf16[512,1024]{1,0:T(8,128)(2,1)}, u32[]{:S(2)}) copy-start(bf16[512,1024]{1,0:T(8,128)(2,1)} %param.4) | copy-start | bytes 3145732
Sparse Core Ops, SparseCore 0:
  597.8 160.8 all-gather.2
